TPU v7x, 32 devices: a whole 2x2x4 slice. The times are simulated.
32 devices in a mesh: groups: 2 (over y), patch: 8 (over z, x), head: 2 (over core).
Axes of the slice: x: 2, y: 2, z: 4, core: 2. Of those that a mesh axis runs over, the one named last changes fastest.
Arguments:
- queries: bfloat16 [2, 256, 1536], P(None, ('groups', 'patch'), 'head'), parts along dimension 1, may hold values from -15 to 15
- stale_pairs: bfloat16 [2, 320, 1536], P(None, ('groups', 'patch'), 'head'), parts along dimension 1, may hold values from -6 to 6
- step_pairs: bfloat16 [2, 2, 320, 1536], P(None, None, ('groups', 'patch'), 'head'), parts along dimension 2, may hold values from -6 to 6
- hidden: bfloat16 [256, 3072], P(('groups', 'patch'), 'head'), parts along dimension 0, may hold values from -3 to 3
- out_weight: bfloat16 [1536, 3072], P('head'), may hold values from -0.15625 to 0.15625
- gate_table: bfloat16 [28, 3072], replicated, may hold values from -4 to 4
- t_index: int32 [4], P('groups'), parts along dimension 0, may hold values from 0 to 27
- text_len: int32 [2], P('groups'), parts along dimension 0, may hold values from 1 to 32
Outputs:
- final_latents: bfloat16 [256, 3072], P(('groups', 'patch', 'head')), parts along dimension 0
There are 2 independent parts, one for each index of `groups`. A program takes and returns all parts, laid end to end along the dimension named above; an argument that names none is the same for every part. Nothing has to cross between parts.
All inputs are finite; a program needn't handle non-finite values.
Results may differ from a plain program's by a relative error of at most 0.0065.
Values may be sent and summed in bfloat16 or wider, within the bound.
A program may use at most 128 MiB of HBM per device.

v0:
```python
import jax
import jax.numpy as jnp
from jax import lax
from jax.sharding import PartitionSpec as P

HDIM = 128


def attend(query_rows, key_rows, value_rows, usable):
    count = query_rows.shape[0]
    total = key_rows.shape[0]
    heads_here = query_rows.shape[1] // HDIM
    qs = query_rows.reshape(count, heads_here, HDIM)
    ks = key_rows.reshape(total, heads_here, HDIM)
    vs = value_rows.reshape(total, heads_here, HDIM)
    scores = jnp.einsum("qhd,khd->hqk", qs, ks, preferred_element_type=jnp.float32) * (
        1.0 / HDIM**0.5
    )
    scores = jnp.where(usable[None, None, :], scores, jnp.float32(-1e30))
    top = jnp.max(scores, axis=2, keepdims=True)
    expo = jnp.exp(scores - top)
    weights = (expo / jnp.sum(expo, axis=2, keepdims=True)).astype(jnp.bfloat16)
    mixed = jnp.einsum("hqk,khd->qhd", weights, vs, preferred_element_type=jnp.float32)
    return mixed.reshape(count, heads_here * HDIM).astype(jnp.bfloat16)


def per_device(queries, stale_pairs, step_pairs, hidden, out_weight, gate_table, t_index, text_len):
    strip_rows = stale_pairs.shape[1]
    lat_rows = queries.shape[1]
    text_rows = strip_rows - lat_rows
    strip_count = lax.axis_size("patch")
    strip_index = lax.axis_index("patch")
    head_index = lax.axis_index("head")
    head_count = lax.axis_size("head")
    total = strip_rows * strip_count
    positions = jnp.arange(total, dtype=jnp.int32)
    within = positions % strip_rows
    holder = positions // strip_rows
    usable = (within < lat_rows) | (holder * text_rows + within - lat_rows < text_len[0])
    old_sets = lax.all_gather(stale_pairs, "patch", axis=1, tiled=True)
    first_sets = lax.all_gather(step_pairs[0], "patch", axis=1, tiled=True)
    remote_sets = (old_sets, first_sets)
    model_width = out_weight.shape[1]
    col_width = model_width // head_count

    def project(section):
        pairs = lax.dynamic_update_slice_in_dim(
            remote_sets[section], step_pairs[section], strip_index * strip_rows, axis=1
        )
        attended = attend(queries[section], pairs[0], pairs[1], usable)
        return jnp.dot(attended, out_weight, preferred_element_type=jnp.float32)

    state = hidden.astype(jnp.float32)
    first_proj = lax.psum_scatter(
        project(0).astype(jnp.bfloat16), "head", scatter_dimension=1, tiled=True
    ).astype(jnp.float32)
    gate_row = gate_table[t_index[0]].astype(jnp.float32)
    state = (
        state
        + lax.dynamic_slice_in_dim(gate_row, head_index * col_width, col_width, 0)[None, :]
        * first_proj
    )
    moved = lax.all_to_all(state, "head", split_axis=0, concat_axis=1, tiled=True)
    last_proj = lax.psum_scatter(project(1), "head", scatter_dimension=0, tiled=True)
    gate_full = gate_table[t_index[1]].astype(jnp.float32)
    return (moved + gate_full[None, :] * last_proj).astype(jnp.bfloat16)


def solution(mesh):
    return jax.shard_map(
        per_device,
        mesh=mesh,
        in_specs=(
            P(None, ("groups", "patch"), "head"),
            P(None, ("groups", "patch"), "head"),
            P(None, None, ("groups", "patch"), "head"),
            P(("groups", "patch"), "head"),
            P("head", None),
            P(),
            P("groups"),
            P("groups"),
        ),
        out_specs=P(("groups", "patch", "head"), None),
        check_vma=False,
    )
```

profile of v0, /device:TPU:0, one launch (start us, length us, event | category | flops | bytes accessed | tf_op | source)
XLA Modules:
  0.0 112.2 jit_solution(2523433137556579357)
XLA Ops:
  6.5 0.0 reduce-scatter.3.cloned.1.call-start
  6.5 0.9 slice_bitcast_fusion
  7.4 33.0 %all-gather = bf16[1,2,160,768]{3,1,0,2:T(2,128)(2,1)S(1)} all-gather(bf16[1,2,20,768]{3,1,0,2:T(2,128)(2,1)S(1)} %slice_bitcast_fusion), channel_id=2, replica_groups=mesh['groups'=2,'patch'=8,'head'=2] {'patch'}, dimensions={2}, use_global_device_ids=true | all-gather | bytes 552960 | tf_op jit(solution)/shard_map/all_gather | solution.py:41
  40.4 31.4 %all_gather.6 = bf16[2,160,768]{2,0,1:T(2,128)(2,1)S(1)} all-gather(bf16[2,20,768]{2,0,1:T(2,128)(2,1)} %param.9), channel_id=1, replica_groups=mesh['groups'=2,'patch'=8,'head'=2] {'patch'}, dimensions={1}, use_global_device_ids=true | all-gather | bytes 552960 | tf_op jit(solution)/shard_map/all_gather | solution.py:40
  71.7 0.8 fusion.33
  72.5 0.1 reshape_squeeze.20
  73.2 1.0 bitcast_dynamic-update-slice_fusion
  74.2 5.2 %slice_reduce_fusion.1 = (bf16[160,768]{1,0:T(8,128)(2,1)S(1)}, bf16[160,768]{1,0:T(8,128)(2,1)S(1)}, bf16[160,768]{1,0:T(8,128)(2,1)S(1)}, bf16[160,768]{1,0:T(8,128)(2,1)S(1)}) fusion(bf16[2,160,768]{2,0,1:T(2,128)(2,1)S(1)} %get-tuple-element.9, bf16[2,160,768]{2,0,1:T(2,128)(2,1)S(1)} %get-tuple-element.10), kind=kLoop, calls=%fused_computation.18 | loop fusion | bytes 1966080 | tf_op jit(solution)/shard_map/slice | solution.py:50
  79.3 0.4 fusion.35
  79.8 0.2 fusion.10
  80.0 0.0 copy-start.1
  80.0 0.0 copy-start
  80.0 3.7 %convolution_convert_fusion = bf16[16,3072]{1,0:T(8,128)(2,1)} fusion(bf16[768,3072]{1,0:T(8,128)(2,1)} %param.12, bf16[6,2,8,128]{3,2,1,0:T(8,128)(2,1)S(1)} %fusion.10), kind=kOutput, calls=%fused_computation.2 | convolution fusion | flops 75546624 | bytes 4841472 | tf_op jit(solution)/shard_map/dot_general | solution.py:51
  83.7 0.0 reduce-scatter.3.cloned.1.call-update
  83.8 0.0 reduce-scatter.5.cloned.1.call-start
  83.8 0.1 reshape_squeeze.23
  83.9 0.4 fusion.36
  84.3 0.2 fusion.11
  84.5 3.7 %fusion.22 = f32[16,3072]{1,0:T(8,128)} fusion(bf16[768,3072]{1,0:T(8,128)(2,1)} %param.12, bf16[6,2,8,128]{3,2,1,0:T(8,128)(2,1)S(1)} %fusion.11), kind=kOutput, calls=%fused_computation.38 | convolution fusion | flops 75497472 | bytes 4939776 | tf_op jit(solution)/shard_map/dot_general | solution.py:51
  88.3 0.0 reduce-scatter.5.cloned.1.call-update
  88.3 0.0 copy-done.1
  88.3 0.6 fusion.34
  92.5 0.8 dynamic-slice_convert_fusion
  93.4 0.8 fusion.29
  94.2 0.0 reduce-scatter.3.cloned.1.call-done
  94.2 0.0 copy-done
  94.2 0.8 add_bitcast_fusion
  95.1 3.8 %all_to_all.19 = f32[2,8,1536]{2,1,0:T(8,128)S(1)} all-to-all(f32[2,8,1536]{2,1,0:T(8,128)S(1)} %add_bitcast_fusion), channel_id=1, replica_groups=mesh['groups'=2,'patch'=8,'head'=2] {'head'}, dimensions={0} | all-to-all | bytes 196608 | tf_op jit(solution)/shard_map/all_to_all | solution.py:63
  98.9 5.0 %reduce-scatter.5.cloned.1.call-done = f32[8,3072]{1,0:T(8,128)} async-done(((f32[16,3072]{1,0:T(8,128)}), f32[8,3072]{1,0:T(8,128)}) %reduce-scatter.5.cloned.1.call-update) | async-done | bytes 98320 | tf_op jit(solution)/shard_map/reduce_scatter | solution.py:64
  103.8 1.5 %add_convert_fusion = bf16[8,3072]{1,0:T(8,128)(2,1)} fusion(f32[8,3072]{1,0:T(8,128)S(1)} %bitcast.74, f32[8,3072]{1,0:T(8,128)} %reduce-scatter.5.cloned.1.call-done, f32[3072]{0:T(1024)S(1)} %bitcast.75), kind=kLoop, calls=%fused_computation.29 | loop fusion | flops 73728 | bytes 258048 | tf_op jit(solution)/shard_map/convert_element_type | solution.py:66
  (1 shorter events, 0.0 us)
Async XLA Ops:
  6.5 87.7 %reduce-scatter.3.cloned.1.call-start = ((), (), s32[]{:S(2)}) async-start(), calls=%async_computation.3 | async-start | bytes 147456 | tf_op jit(solution)/shard_map/reduce_scatter | solution.py:54
  80.0 8.3 %copy-start.1 = (s32[2]{0:T(128)S(1)}, s32[2]{0:T(128)}, u32[]{:S(2)}) copy-start(s32[2]{0:T(128)} %param.14) | copy-start | bytes 28
  80.0 14.2 %copy-start = (bf16[16,1536]{1,0:T(8,128)(2,1)S(1)}, bf16[16,1536]{1,0:T(8,128)(2,1)}, u32[]{:S(2)}) copy-start(bf16[16,1536]{1,0:T(8,128)(2,1)} %param.11) | copy-start | bytes 147460
  83.8 20.1 %reduce-scatter.5.cloned.1.call-start = ((), (), s32[]{:S(2)}) async-start(), calls=%async_computation.4 | async-start | bytes 294912 | tf_op jit(solution)/shard_map/reduce_scatter | solution.py:64
Sparse Core Ops, SparseCore 0:
  83.9 8.8 reduce-scatter.2
  95.1 8.7 reduce-scatter.4
where the time goes:
time: 113 us; the launch traced here: 112 us
  blocking collectives  68.1 us (60%)
  between operations  17.8 us (16%)
  matrix products  8.77 us (8%)
  local copies, waits for them, and re-layouts  8.44 us (7%)
  waiting for transfers between devices  5.03 us (4%)
  other arithmetic  4.01 us (4%)
    all_gather x1, blocking collectives, per_device(): first_sets = lax.all_gather(step_pairs[0], 'patch', axis=1, tiled=True)  33 us
    all_gather x1, blocking collectives, per_device(): old_sets = lax.all_gather(stale_pairs, 'patch', axis=1, tiled=True)  31.4 us
    dot_general x2, matrix products, project(): return jnp.dot(attended, out_weight, preferred_element_type=jnp.float32)  7.5 us
    slice x2, local copies, waits for them, and re-layouts, project(): attended = attend(queries[section], pairs[0], pairs[1], usable)  5.91 us
    reduce_scatter x1, waiting for transfers between devices, per_device(): lax.psum_scatter(project(1), 'head', scatter_dimension=0, tiled=True)  4.98 us
    all_to_all x1, blocking collectives, per_device(): lax.all_to_all(state, 'head', split_axis=0, concat_axis=1, tiled=True)  3.79 us
  transfers between devices with their start and end apart: 2, of which 1 were waited for; matrix products, arithmetic and copies ran while one was open for 7% of the time, Pallas kernels for 0%

commit v1 on v0

--- a/solution.py
+++ b/solution.py
@@ -37,7 +37,14 @@
     within = positions % strip_rows
     holder = positions // strip_rows
     usable = (within < lat_rows) | (holder * text_rows + within - lat_rows < text_len[0])
-    old_sets = lax.all_gather(stale_pairs, "patch", axis=1, tiled=True)
+    ring = [stale_pairs]
+    for hop in range(7):
+        ring.append(lax.ppermute(ring[-1], "patch", [(dev, (dev + 1) % 8) for dev in range(8)]))
+    old_sets = jnp.roll(
+        jnp.concatenate(ring[::-1], axis=1),
+        (lax.axis_index("patch") + 1) * ring[0].shape[1],
+        axis=1,
+    )
     first_sets = lax.all_gather(step_pairs[0], "patch", axis=1, tiled=True)
     remote_sets = (old_sets, first_sets)
     model_width = out_weight.shape[1]

time: 113 us -> 126 us (1.12)
  waiting for transfers between devices: 5.03 us -> 41.5 us
  blocking collectives: 68.1 us -> 35.4 us
  starting transfers between devices: 0.04 us -> 4.96 us
  local copies, waits for them, and re-layouts: 8.44 us -> 12 us
    ppermute x0 -> x7, waiting for transfers between devices: none -> 32.7 us  [per_device(): lax.ppermute(ring[-1], 'patch', [(dev, (dev + 1) % 8) for dev in range(8)])]
    all_gather x1 -> x0, blocking collectives: 31.4 us -> none  [per_device(): old_sets = lax.all_gather(stale_pairs, 'patch', axis=1, tiled=True)]
    ppermute x0 -> x7, starting transfers between devices: none -> 4.92 us  [per_device(): lax.ppermute(ring[-1], 'patch', [(dev, (dev + 1) % 8) for dev in range(8)])]
    unnamed x4 -> x18, local copies, waits for them, and re-layouts: 0.01 us -> 2.5 us
    reduce_scatter x1, waiting for transfers between devices: 0.02 us -> 2.3 us  [per_device(): lax.psum_scatter(project(0).astype(jnp.bfloat16), 'head', scatter_dimensi...]
    reduce_scatter x1, waiting for transfers between devices: 4.98 us -> 6.39 us  [per_device(): lax.psum_scatter(project(1), 'head', scatter_dimension=0, tiled=True)]
    all_gather x1, blocking collectives: 33 us -> 31.6 us  [per_device(): first_sets = lax.all_gather(step_pairs[0], 'patch', axis=1, tiled=True)]
  transfers between devices with their start and end apart: 2 -> 9, of which waited for: 1 -> 8; matrix products, arithmetic and copies ran while one was open for 7% -> 8% of each run, Pallas kernels for 0% -> 0%
where the time goes in v1:
time: 126 us; the launch traced here: 125 us
  waiting for transfers between devices  41.5 us (33%)
  blocking collectives  35.4 us (28%)
  between operations  18.2 us (14%)
  local copies, waits for them, and re-layouts  12 us (10%)
  matrix products  8.76 us (7%)
  starting transfers between devices  4.96 us (4%)
  other arithmetic  4.01 us (3%)
    ppermute x7, waiting for transfers between devices, per_device(): lax.ppermute(ring[-1], 'patch', [(dev, (dev + 1) % 8) for dev in range(8)])  32.7 us
    all_gather x1, blocking collectives, per_device(): first_sets = lax.all_gather(step_pairs[0], 'patch', axis=1, tiled=True)  31.6 us
    dot_general x2, matrix products, project(): return jnp.dot(attended, out_weight, preferred_element_type=jnp.float32)  7.49 us
    reduce_scatter x1, waiting for transfers between devices, per_device(): lax.psum_scatter(project(1), 'head', scatter_dimension=0, tiled=True)  6.39 us
    slice x2, local copies, waits for them, and re-layouts, project(): attended = attend(queries[section], pairs[0], pairs[1], usable)  5.87 us
    ppermute x7, starting transfers between devices, per_device(): lax.ppermute(ring[-1], 'patch', [(dev, (dev + 1) % 8) for dev in range(8)])  4.92 us
    all_to_all x1, blocking collectives, per_device(): lax.all_to_all(state, 'head', split_axis=0, concat_axis=1, tiled=True)  3.79 us
  transfers between devices with their start and end apart: 9, of which 8 were waited for; matrix products, arithmetic and copies ran while one was open for 8% of the time, Pallas kernels for 0%

profile of v1, /device:TPU:0, one launch (start us, length us, event | category | flops | bytes accessed | tf_op | source)
XLA Modules:
  0.0 124.8 jit_solution(5311664434787692759)
XLA Ops:
  6.5 3.0 %collective-permute-start = (bf16[2,20,768]{2,0,1:T(2,128)(2,1)}, bf16[2,20,768]{2,0,1:T(2,128)(2,1)S(1)}, u32[]{:S(2)}, u32[]{:S(2)}) collective-permute-start(bf16[2,20,768]{2,0,1:T(2,128)(2,1)} %param.9), channel_id=1, source_target_pairs={{0,2},{2,4},{4,6},{6,8},{8,10},{10,12},{12,14},{14,0},{1,3},{3,5},... | collective-permute-start | bytes 184328 | tf_op jit(solution)/shard_map/ppermute | solution.py:42
  9.5 5.4 %collective-permute-done = bf16[2,20,768]{2,0,1:T(2,128)(2,1)S(1)} collective-permute-done((bf16[2,20,768]{2,0,1:T(2,128)(2,1)}, bf16[2,20,768]{2,0,1:T(2,128)(2,1)S(1)}, u32[]{:S(2)}, u32[]{:S(2)}) %collective-permute-start) | collective-permute-done | bytes 61472 | tf_op jit(solution)/shard_map/ppermute | solution.py:42
  15.0 1.3 %fusion.34 = (s32[1]{0:T(128)}, s32[1]{0:T(128)}) fusion(s32[2]{0:T(128)} %param.14), kind=kLoop, calls=%fused_computation.75 | loop fusion | bytes 16 | tf_op jit(solution)/shard_map/slice | solution.py:72
  18.2 3.6 %collective-permute-done.1 = bf16[2,20,768]{2,0,1:T(2,128)(2,1)S(1)} collective-permute-done((bf16[2,20,768]{2,0,1:T(2,128)(2,1)S(1)}, bf16[2,20,768]{2,0,1:T(2,128)(2,1)S(1)}, u32[]{:S(2)}, u32[]{:S(2)}) %collective-permute-start.1) | collective-permute-done | bytes 61472 | tf_op jit(solution)/shard_map/ppermute | solution.py:42
  21.9 0.8 dynamic-slice_convert_fusion
  22.7 6.1 %collective-permute-done.2 = bf16[2,20,768]{2,0,1:T(2,128)(2,1)S(1)} collective-permute-done((bf16[2,20,768]{2,0,1:T(2,128)(2,1)S(1)}, bf16[2,20,768]{2,0,1:T(2,128)(2,1)S(1)}, u32[]{:S(2)}, u32[]{:S(2)}) %collective-permute-start.2) | collective-permute-done | bytes 61472 | tf_op jit(solution)/shard_map/ppermute | solution.py:42
  28.8 0.9 slice_bitcast_fusion
  29.7 6.0 %collective-permute-done.3 = bf16[2,20,768]{2,0,1:T(2,128)(2,1)S(1)} collective-permute-done((bf16[2,20,768]{2,0,1:T(2,128)(2,1)S(1)}, bf16[2,20,768]{2,0,1:T(2,128)(2,1)S(1)}, u32[]{:S(2)}, u32[]{:S(2)}) %collective-permute-start.3) | collective-permute-done | bytes 61472 | tf_op jit(solution)/shard_map/ppermute | solution.py:42
  35.7 0.8 fusion.33
  36.5 6.5 %collective-permute-done.4 = bf16[2,20,768]{2,0,1:T(2,128)(2,1)S(1)} collective-permute-done((bf16[2,20,768]{2,0,1:T(2,128)(2,1)S(1)}, bf16[2,20,768]{2,0,1:T(2,128)(2,1)S(1)}, u32[]{:S(2)}, u32[]{:S(2)}) %collective-permute-start.4) | collective-permute-done | bytes 61472 | tf_op jit(solution)/shard_map/ppermute | solution.py:42
  43.0 31.6 %all-gather = bf16[1,2,160,768]{3,1,0,2:T(2,128)(2,1)S(1)} all-gather(bf16[1,2,20,768]{3,1,0,2:T(2,128)(2,1)S(1)} %slice_bitcast_fusion), channel_id=2, replica_groups=mesh['groups'=2,'patch'=8,'head'=2] {'patch'}, dimensions={2}, use_global_device_ids=true | all-gather | bytes 552960 | tf_op jit(solution)/shard_map/all_gather | solution.py:48
  75.9 0.1 reshape_squeeze.23
  76.7 0.1 reshape_squeeze.20
  77.4 0.8 fusion.29
  78.3 1.9 %collective-permute-start.6 = (bf16[2,20,768]{2,0,1:T(2,128)(2,1)S(1)}, bf16[2,20,768]{2,0,1:T(2,128)(2,1)S(1)}, u32[]{:S(2)}, u32[]{:S(2)}) collective-permute-start(bf16[2,20,768]{2,0,1:T(2,128)(2,1)S(1)} %collective-permute-done.5), channel_id=1, source_target_pairs={{0,2},{2,4},{4,6},{6,8},{8,10},{10,12},{12,14},{14,0},{1,3},{3,5},... | collective-permute-start | bytes 184328 | tf_op jit(solution)/shard_map/ppermute | solution.py:42
  80.2 5.0 %collective-permute-done.6 = bf16[2,20,768]{2,0,1:T(2,128)(2,1)S(1)} collective-permute-done((bf16[2,20,768]{2,0,1:T(2,128)(2,1)S(1)}, bf16[2,20,768]{2,0,1:T(2,128)(2,1)S(1)}, u32[]{:S(2)}, u32[]{:S(2)}) %collective-permute-start.6) | collective-permute-done | bytes 61472 | tf_op jit(solution)/shard_map/ppermute | solution.py:42
  85.3 0.1 constant_dynamic-update-slice_fusion.14
  85.3 0.1 constant_dynamic-update-slice_fusion.13
  85.4 0.1 constant_dynamic-update-slice_fusion.12
  85.5 0.1 constant_dynamic-update-slice_fusion.11
  85.5 0.1 constant_dynamic-update-slice_fusion.10
  85.6 0.1 constant_dynamic-update-slice_fusion.9
  85.6 0.9 constant_dynamic-update-slice_fusion.8
  86.5 0.1 constant_dynamic-update-slice_fusion.7
  86.6 0.1 constant_dynamic-update-slice_fusion.6
  86.6 0.1 constant_dynamic-update-slice_fusion.5
  86.7 0.1 constant_dynamic-update-slice_fusion.4
  86.8 0.1 constant_dynamic-update-slice_fusion.3
  86.8 0.1 constant_dynamic-update-slice_fusion.2
  86.9 0.1 constant_dynamic-update-slice_fusion.1
  86.9 0.9 constant_dynamic-update-slice_fusion
  87.8 0.3 constant_dynamic-slice_fusion
  88.2 1.0 bitcast_dynamic-update-slice_fusion.1
  89.2 5.1 %slice_reduce_fusion.1 = (bf16[160,768]{1,0:T(8,128)(2,1)S(1)}, bf16[160,768]{1,0:T(8,128)(2,1)S(1)}, bf16[160,768]{1,0:T(8,128)(2,1)S(1)}, bf16[160,768]{1,0:T(8,128)(2,1)S(1)}) fusion(bf16[2,160,768]{2,0,1:T(2,128)(2,1)S(1)} %get-tuple-element.9, bf16[2,160,768]{2,0,1:T(2,128)(2,1)S(1)} %get-tuple-element.10), kind=kLoop, calls=%fused_computation.18 | loop fusion | bytes 1966080 | tf_op jit(solution)/shard_map/slice | solution.py:57
  94.3 0.4 fusion.35
  94.7 0.2 fusion.10
  94.9 3.7 %convolution_convert_fusion = bf16[16,3072]{1,0:T(8,128)(2,1)} fusion(bf16[768,3072]{1,0:T(8,128)(2,1)} %param.12, bf16[6,2,8,128]{3,2,1,0:T(8,128)(2,1)S(1)} %fusion.10), kind=kOutput, calls=%fused_computation.2 | convolution fusion | flops 75546624 | bytes 4841472 | tf_op jit(solution)/shard_map/dot_general | solution.py:58
  98.7 0.0 reduce-scatter.3.cloned.1.call-update
  98.7 0.0 reduce-scatter.5.cloned.1.call-start
  98.7 0.4 fusion.36
  99.1 0.2 fusion.11
  99.4 3.8 %fusion.22 = f32[16,3072]{1,0:T(8,128)} fusion(bf16[768,3072]{1,0:T(8,128)(2,1)} %param.12, bf16[6,2,8,128]{3,2,1,0:T(8,128)(2,1)S(1)} %fusion.11), kind=kOutput, calls=%fused_computation.54 | convolution fusion | flops 75497472 | bytes 4939776 | tf_op jit(solution)/shard_map/dot_general | solution.py:58
  103.1 0.0 reduce-scatter.5.cloned.1.call-update
  103.1 2.3 %reduce-scatter.3.cloned.1.call-done = bf16[16,1536]{1,0:T(8,128)(2,1)} async-done(((bf16[16,3072]{1,0:T(8,128)(2,1)}), bf16[16,1536]{1,0:T(8,128)(2,1)}) %reduce-scatter.3.cloned.1.call-update) | async-done | bytes 49168 | tf_op jit(solution)/shard_map/reduce_scatter | solution.py:61
  105.4 0.8 add_bitcast_fusion
  106.3 3.8 %all_to_all.19 = f32[2,8,1536]{2,1,0:T(8,128)S(1)} all-to-all(f32[2,8,1536]{2,1,0:T(8,128)S(1)} %add_bitcast_fusion), channel_id=1, replica_groups=mesh['groups'=2,'patch'=8,'head'=2] {'head'}, dimensions={0} | all-to-all | bytes 196608 | tf_op jit(solution)/shard_map/all_to_all | solution.py:70
  110.1 6.4 %reduce-scatter.5.cloned.1.call-done = f32[8,3072]{1,0:T(8,128)} async-done(((f32[16,3072]{1,0:T(8,128)}), f32[8,3072]{1,0:T(8,128)}) %reduce-scatter.5.cloned.1.call-update) | async-done | bytes 98320 | tf_op jit(solution)/shard_map/reduce_scatter | solution.py:71
  116.5 1.5 %add_convert_fusion = bf16[8,3072]{1,0:T(8,128)(2,1)} fusion(f32[8,3072]{1,0:T(8,128)S(1)} %bitcast.75, f32[8,3072]{1,0:T(8,128)} %reduce-scatter.5.cloned.1.call-done, f32[3072]{0:T(1024)S(1)} %bitcast.76), kind=kLoop, calls=%fused_computation.29 | loop fusion | flops 73728 | bytes 258048 | tf_op jit(solution)/shard_map/convert_element_type | solution.py:73
  (11 shorter events, 0.1 us)
Async XLA Ops:
  6.5 98.9 %reduce-scatter.3.cloned.1.call-start = ((), (), s32[]{:S(2)}) async-start(), calls=%async_computation.3 | async-start | bytes 147456 | tf_op jit(solution)/shard_map/reduce_scatter | solution.py:61
  6.5 8.4 %collective-permute-start = (bf16[2,20,768]{2,0,1:T(2,128)(2,1)}, bf16[2,20,768]{2,0,1:T(2,128)(2,1)S(1)}, u32[]{:S(2)}, u32[]{:S(2)}) collective-permute-start(bf16[2,20,768]{2,0,1:T(2,128)(2,1)} %param.9), channel_id=1, source_target_pairs={{0,2},{2,4},{4,6},{6,8},{8,10},{10,12},{12,14},{14,0},{1,3},{3,5},... | collective-permute-start | bytes 184328 | tf_op jit(solution)/shard_map/ppermute | solution.py:42
  15.0 6.9 %collective-permute-start.1 = (bf16[2,20,768]{2,0,1:T(2,128)(2,1)S(1)}, bf16[2,20,768]{2,0,1:T(2,128)(2,1)S(1)}, u32[]{:S(2)}, u32[]{:S(2)}) collective-permute-start(bf16[2,20,768]{2,0,1:T(2,128)(2,1)S(1)} %collective-permute-done), channel_id=1, source_target_pairs={{0,2},{2,4},{4,6},{6,8},{8,10},{10,12},{12,14},{14,0},{1,3},{3,5},... | collective-permute-start | bytes 184328 | tf_op jit(solution)/shard_map/ppermute | solution.py:42
  21.9 6.9 %collective-permute-start.2 = (bf16[2,20,768]{2,0,1:T(2,128)(2,1)S(1)}, bf16[2,20,768]{2,0,1:T(2,128)(2,1)S(1)}, u32[]{:S(2)}, u32[]{:S(2)}) collective-permute-start(bf16[2,20,768]{2,0,1:T(2,128)(2,1)S(1)} %collective-permute-done.1), channel_id=1, source_target_pairs={{0,2},{2,4},{4,6},{6,8},{8,10},{10,12},{12,14},{14,0},{1,3},{3,5},... | collective-permute-start | bytes 184328 | tf_op jit(solution)/shard_map/ppermute | solution.py:42
  28.8 6.9 %collective-permute-start.3 = (bf16[2,20,768]{2,0,1:T(2,128)(2,1)S(1)}, bf16[2,20,768]{2,0,1:T(2,128)(2,1)S(1)}, u32[]{:S(2)}, u32[]{:S(2)}) collective-permute-start(bf16[2,20,768]{2,0,1:T(2,128)(2,1)S(1)} %collective-permute-done.2), channel_id=1, source_target_pairs={{0,2},{2,4},{4,6},{6,8},{8,10},{10,12},{12,14},{14,0},{1,3},{3,5},... | collective-permute-start | bytes 184328 | tf_op jit(solution)/shard_map/ppermute | solution.py:42
  35.7 7.3 %collective-permute-start.4 = (bf16[2,20,768]{2,0,1:T(2,128)(2,1)S(1)}, bf16[2,20,768]{2,0,1:T(2,128)(2,1)S(1)}, u32[]{:S(2)}, u32[]{:S(2)}) collective-permute-start(bf16[2,20,768]{2,0,1:T(2,128)(2,1)S(1)} %collective-permute-done.3), channel_id=1, source_target_pairs={{0,2},{2,4},{4,6},{6,8},{8,10},{10,12},{12,14},{14,0},{1,3},{3,5},... | collective-permute-start | bytes 184328 | tf_op jit(solution)/shard_map/ppermute | solution.py:42
  43.0 35.3 %collective-permute-start.5 = (bf16[2,20,768]{2,0,1:T(2,128)(2,1)S(1)}, bf16[2,20,768]{2,0,1:T(2,128)(2,1)S(1)}, u32[]{:S(2)}, u32[]{:S(2)}) collective-permute-start(bf16[2,20,768]{2,0,1:T(2,128)(2,1)S(1)} %collective-permute-done.4), channel_id=1, source_target_pairs={{0,2},{2,4},{4,6},{6,8},{8,10},{10,12},{12,14},{14,0},{1,3},{3,5},... | collective-permute-start | bytes 184328 | tf_op jit(solution)/shard_map/ppermute | solution.py:42
  78.3 7.0 %collective-permute-start.6 = (bf16[2,20,768]{2,0,1:T(2,128)(2,1)S(1)}, bf16[2,20,768]{2,0,1:T(2,128)(2,1)S(1)}, u32[]{:S(2)}, u32[]{:S(2)}) collective-permute-start(bf16[2,20,768]{2,0,1:T(2,128)(2,1)S(1)} %collective-permute-done.5), channel_id=1, source_target_pairs={{0,2},{2,4},{4,6},{6,8},{8,10},{10,12},{12,14},{14,0},{1,3},{3,5},... | collective-permute-start | bytes 184328 | tf_op jit(solution)/shard_map/ppermute | solution.py:42
  94.9 10.5 %copy-start = (bf16[16,1536]{1,0:T(8,128)(2,1)S(1)}, bf16[16,1536]{1,0:T(8,128)(2,1)}, u32[]{:S(2)}) copy-start(bf16[16,1536]{1,0:T(8,128)(2,1)} %param.11) | copy-start | bytes 147460
  98.7 17.8 %reduce-scatter.5.cloned.1.call-start = ((), (), s32[]{:S(2)}) async-start(), calls=%async_computation.4 | async-start | bytes 294912 | tf_op jit(solution)/shard_map/reduce_scatter | solution.py:71
Sparse Core Ops, SparseCore 0:
  98.8 6.6 reduce-scatter.2
  107.7 8.7 reduce-scatter.4
